TPU v7x, 32 devices: a whole 2x2x4 slice. The times are simulated.
32 devices in a mesh: groups: 2 (over x), tok: 16 (over z, y, core).
Axes of the slice: x: 2, y: 2, z: 4, core: 2. Of those that a mesh axis runs over, the one named last changes fastest.
Arguments:
- latents: bfloat16 [2304, 1536], P(('groups', 'tok')), parts along dimension 0, may hold values from -6 to 6
- fresh_noise: bfloat16 [2304, 1536], P(('groups', 'tok')), parts along dimension 0, may hold values from -6 to 6
- levels: int32 [4], replicated, may hold values from 50 to 996, as said below
- time_weight: bfloat16 [256, 3072], replicated, may hold values from -0.375 to 0.375
- w_query: bfloat16 [1536, 768], replicated, may hold values from -1 to 1
- w_key: bfloat16 [1536, 768], replicated, may hold values from -10 to 10
- w_value: bfloat16 [1536, 768], replicated, may hold values from -0.15625 to 0.15625
- w_out: bfloat16 [768, 1536], replicated, may hold values from -0.21875 to 0.21875
Outputs:
- stepped: bfloat16 [2, 2304, 1536], P(None, ('groups', 'tok')), parts along dimension 1
- velocity: bfloat16 [2, 2304, 1536], P(None, ('groups', 'tok')), parts along dimension 1
There are 2 independent parts, one for each index of `groups`. A program takes and returns all parts, laid end to end along the dimension named above; an argument that names none is the same for every part. Nothing has to cross between parts.
Inputs may be any that keep to these rules, and one draw needn't show every extreme that they name: `levels`: strictly increasing over sections.
All inputs are finite; a program needn't handle non-finite values.
Results may differ from a plain program's by a relative error of at most 0.0095.
Values may be sent and summed in bfloat16 or wider, within the bound.
No kernel may reach another device: no remote copies, remote signals or barrier semaphores. Data moves between devices by JAX's collectives and lax.ppermute only.
A program may use at most 128 MiB of HBM per device.

v0:
```python
import math
import jax
import jax.numpy as jnp
from jax import lax
from jax.sharding import PartitionSpec as P

D = 1536
HEADS = 6
HEAD_DIM = 128
TFREQ = 256
SECTIONS = 4
epsilon = 1e-06


def shifted(block, axis, distance):
    devices = range(lax.axis_size(axis))
    route = [(i - distance, i) for i in devices if i - distance in devices]
    return lax.ppermute(block, axis, route)


def embed_level(level_value, time_weight):
    half_width = TFREQ // 2
    frequency = jnp.exp(-math.log(10000.0) * jnp.arange(half_width, dtype=jnp.float32) / half_width)
    angles = level_value.astype(jnp.float32) * frequency
    embedding = jnp.concatenate([jnp.cos(angles), jnp.sin(angles)])[None, :]
    modulated = jnp.dot(
        embedding, time_weight.astype(jnp.float32), precision=lax.Precision.HIGHEST
    )[0]
    return (modulated[:D], modulated[D:])


def body(latents, fresh_noise, levels, time_weight, w_query, w_key, w_value, w_out):
    local_rows = latents.shape[0]
    per_section = lax.axis_size("tok") // SECTIONS
    span_rows = local_rows * per_section
    my_block = lax.axis_index("tok") // per_section
    section_ids = jnp.arange(SECTIONS, dtype=jnp.int32)
    my_level = jnp.sum(jnp.where(section_ids == my_block, levels, 0))
    prev_level = jnp.sum(jnp.where(section_ids == my_block - 1, levels, 0))
    step_size = (prev_level - my_level).astype(jnp.float32) / 1000.0
    shift_vec, scale_vec = embed_level(my_level, time_weight)

    def denoise_local(rows):
        rows_f = rows.astype(jnp.float32)
        normed = rows_f * lax.rsqrt(jnp.mean(rows_f * rows_f, axis=-1, keepdims=True) + epsilon)
        hidden = (normed * (1.0 + scale_vec) + shift_vec).astype(jnp.bfloat16)
        queries = jnp.dot(hidden, w_query, preferred_element_type=jnp.float32).astype(jnp.bfloat16)
        queries = queries.reshape(local_rows, HEADS, HEAD_DIM)
        local_keys = jnp.dot(hidden, w_key, preferred_element_type=jnp.float32).astype(jnp.bfloat16)
        local_values = jnp.dot(hidden, w_value, preferred_element_type=jnp.float32).astype(
            jnp.bfloat16
        )
        gathered_keys, gathered_values = (
            lax.all_gather(local_keys, "tok", axis=0, tiled=True),
            lax.all_gather(local_values, "tok", axis=0, tiled=True),
        )
        best = jnp.full((HEADS, local_rows), -1e30, jnp.float32)
        count = gathered_keys.shape[0]
        key_blocks = jnp.arange(count, dtype=jnp.int32) // span_rows
        allowed = (key_blocks <= my_block)[None, None, :]
        scores = jnp.einsum(
            "rhd,phd->hrp",
            queries,
            gathered_keys.reshape(count, HEADS, HEAD_DIM),
            preferred_element_type=jnp.float32,
        ) / math.sqrt(HEAD_DIM)
        scores = jnp.where(allowed, scores, -1e30)
        new_best = jnp.maximum(best, jnp.max(scores, axis=-1))
        weights = jnp.where(allowed, jnp.exp(scores - new_best[..., None]), 0.0)
        denominator = jnp.sum(weights, axis=-1)
        summed = jnp.einsum(
            "hrp,phd->hrd",
            weights.astype(jnp.bfloat16),
            gathered_values.reshape(count, HEADS, HEAD_DIM),
            preferred_element_type=jnp.float32,
        )
        result = (new_best, denominator, summed)
        best, denominator, summed = result
        attended = (summed / denominator[..., None]).astype(jnp.bfloat16)
        attended = attended.transpose(1, 0, 2).reshape(local_rows, HEADS * HEAD_DIM)
        moving = jnp.dot(attended, w_out, preferred_element_type=jnp.float32)
        stepped = (rows_f + step_size * moving).astype(jnp.bfloat16)
        return (stepped, moving.astype(jnp.bfloat16))

    first, first_moving = denoise_local(latents)
    incoming = shifted(first, "tok", -per_section)
    second_input = jnp.where(my_block == SECTIONS - 1, fresh_noise, incoming)
    second, second_moving = denoise_local(second_input)
    return (jnp.stack([first, second]), jnp.stack([first_moving, second_moving]))


def solution(mesh):
    return jax.shard_map(
        body,
        mesh=mesh,
        in_specs=(
            P(("groups", "tok"), None),
            P(("groups", "tok"), None),
            P(),
            P(),
            P(),
            P(),
            P(),
            P(),
        ),
        out_specs=(P(None, ("groups", "tok"), None), P(None, ("groups", "tok"), None)),
        check_vma=False,
    )
```

profile of v0, /device:TPU:0, one launch (start us, length us, event | category | flops | bytes accessed | tf_op | source)
XLA Modules:
  0.0 216.5 jit_solution(2579585131314085424)
XLA Ops:
  7.2 0.0 copy-start
  7.2 0.0 copy-start.3
  7.2 0.0 all-gather.5.cloned.1.call-start
  7.3 1.5 fusion.47
  9.4 2.1 fusion.65
  11.5 1.1 fusion.22
  12.6 0.0 copy-done.3
  12.6 2.9 %convolution_convert_fusion.4 = bf16[72,768]{1,0:T(8,128)(2,1)} fusion(bf16[1536,768]{1,0:T(8,128)(2,1)} %param.13, bf16[72,1536]{1,0:T(8,128)(2,1)S(1)} %copy-done.3, f32[1536]{0:T(1024)S(1)} %get-tuple-element.11, f32[1536]{0:T(1024)S(1)} %get-tuple-element.10, f32[72]{0:T(128)S(1)} %add_rsqrt_fusion.1), kind=kOutput, calls=%fused_computation.20 | convolution fusion | flops 170477568 | bytes 2703648 | tf_op jit(solution)/shard_map/dot_general | solution.py:49
  15.5 0.0 all-gather.5.cloned.1.call-update
  15.6 0.0 all-gather.7.cloned.1.call-start
  15.6 2.9 %convolution_convert_fusion.3 = bf16[72,768]{1,0:T(8,128)(2,1)} fusion(bf16[1536,768]{1,0:T(8,128)(2,1)} %param.14, bf16[72,1536]{1,0:T(8,128)(2,1)S(1)} %copy-done.3, f32[1536]{0:T(1024)S(1)} %get-tuple-element.11, f32[1536]{0:T(1024)S(1)} %get-tuple-element.10, f32[72]{0:T(128)S(1)} %add_rsqrt_fusion.1), kind=kOutput, calls=%fused_computation.19 | convolution fusion | flops 170477568 | bytes 2703648 | tf_op jit(solution)/shard_map/dot_general | solution.py:50
  18.5 0.0 all-gather.7.cloned.1.call-update
  18.5 0.0 all-gather.9.cloned.1.call-start
  19.7 2.2 %fusion.12 = bf16[9,6,8,128]{3,2,1,0:T(8,128)(2,1)S(1)} fusion(bf16[1536,768]{1,0:T(8,128)(2,1)} %param.12, bf16[72,1536]{1,0:T(8,128)(2,1)S(1)} %copy-done.3, f32[1536]{0:T(1024)S(1)} %get-tuple-element.11, f32[1536]{0:T(1024)S(1)} %get-tuple-element.10, f32[72]{0:T(128)S(1)} %add_rsqrt_fusion.1), kind=kOutput, calls=%fused_computation.24 | convolution fusion | flops 170477568 | bytes 2703648 | tf_op jit(solution)/shard_map/dot_general | solution.py:47
  22.0 36.7 %all-gather.5.cloned.1.call-done = bf16[1152,768]{1,0:T(8,128)(2,1)} async-done(((bf16[72,768]{1,0:T(8,128)(2,1)}), bf16[1152,768]{1,0:T(8,128)(2,1)}) %all-gather.5.cloned.1.call-update) | async-done | bytes 1769488 | tf_op jit(solution)/shard_map/all_gather | solution.py:54
  58.7 3.9 %copy.16 = bf16[1152,768]{0,1:T(8,128)(2,1)} copy(bf16[1152,768]{1,0:T(8,128)(2,1)} %all-gather.5.cloned.1.call-done) | data formatting | bytes 3538944 | tf_op jit(solution)/shard_map/all_gather | solution.py:54
  62.6 2.1 fusion.59
  64.6 0.0 copy-start.2
  64.6 1.3 copy-done.2
  65.9 0.5 fusion.2
  66.4 34.1 %all-gather.7.cloned.1.call-done = bf16[1152,768]{1,0:T(8,128)(2,1)} async-done(((bf16[72,768]{1,0:T(8,128)(2,1)}), bf16[1152,768]{1,0:T(8,128)(2,1)}) %all-gather.7.cloned.1.call-update) | async-done | bytes 1769488 | tf_op jit(solution)/shard_map/all_gather | solution.py:55
  100.5 3.9 %copy.19 = bf16[1152,768]{0,1:T(8,128)(2,1)} copy(bf16[1152,768]{1,0:T(8,128)(2,1)} %all-gather.7.cloned.1.call-done) | data formatting | bytes 3538944 | tf_op jit(solution)/shard_map/all_gather | solution.py:55
  104.4 3.0 %fusion.11 = bf16[6,9,8,128]{3,2,1,0:T(8,128)(2,1)S(1)} fusion(bf16[1152,6,128]{0,2,1:T(8,128)(2,1)} %bitcast.76, f32[6,72,1152]{2,1,0:T(8,128)} %copy-done.2, f32[6,72]{1,0:T(8,128)S(1)} %broadcast_maximum_fusion.1, pred[1152]{0:T(1024)(128)(4,1)S(1)} %fusion.43, f32[72,6]{0,1:T(8,128)S(1)} %bitcast.80), kind=kOutput, calls=%fused_computation.23 | convolution fusion | flops 129005568 | bytes 3875328 | tf_op jit(solution)/shard_map/hrp,phd->hrd/dot_general | solution.py:71
  107.4 0.0 copy-done
  107.4 0.0 copy-start.4
  107.4 0.5 convert_bitcast_fusion.1
  108.0 1.3 collective-permute-start
  109.3 8.3 %collective-permute-done = bf16[72,1536]{1,0:T(8,128)(2,1)} collective-permute-done((bf16[72,1536]{1,0:T(8,128)(2,1)S(1)}, bf16[72,1536]{1,0:T(8,128)(2,1)}, u32[]{:S(2)}, u32[]{:S(2)}) %collective-permute-start) | collective-permute-done | bytes 221216 | tf_op jit(solution)/shard_map/ppermute | solution.py:18
  117.5 0.0 copy-done.4
  117.5 1.1 fusion.27
  118.7 2.9 %convolution_convert_fusion.1 = bf16[72,768]{1,0:T(8,128)(2,1)} fusion(bf16[1536,768]{1,0:T(8,128)(2,1)} %param.13, bf16[72,1536]{1,0:T(8,128)(2,1)S(1)} %get-tuple-element.5, f32[72]{0:T(128)S(1)} %add_rsqrt_fusion, f32[1536]{0:T(1024)S(1)} %get-tuple-element.11, f32[1536]{0:T(1024)S(1)} %get-tuple-element.10), kind=kOutput, calls=%fused_computation.17 | convolution fusion | flops 170477568 | bytes 2703648 | tf_op jit(solution)/shard_map/dot_general | solution.py:49
  121.6 0.0 all-gather.9.cloned.1.call-update
  121.6 0.0 all-gather.11.cloned.1.call-start
  121.6 2.9 %convolution_convert_fusion = bf16[72,768]{1,0:T(8,128)(2,1)} fusion(bf16[1536,768]{1,0:T(8,128)(2,1)} %param.14, bf16[72,1536]{1,0:T(8,128)(2,1)S(1)} %get-tuple-element.5, f32[72]{0:T(128)S(1)} %add_rsqrt_fusion, f32[1536]{0:T(1024)S(1)} %get-tuple-element.11, f32[1536]{0:T(1024)S(1)} %get-tuple-element.10), kind=kOutput, calls=%fused_computation.16 | convolution fusion | flops 170477568 | bytes 2703648 | tf_op jit(solution)/shard_map/dot_general | solution.py:50
  124.5 0.0 all-gather.11.cloned.1.call-update
  124.6 2.3 %fusion.13 = bf16[9,6,8,128]{3,2,1,0:T(8,128)(2,1)S(1)} fusion(bf16[1536,768]{1,0:T(8,128)(2,1)} %param.12, bf16[72,1536]{1,0:T(8,128)(2,1)S(1)} %get-tuple-element.5, f32[72]{0:T(128)S(1)} %add_rsqrt_fusion, f32[1536]{0:T(1024)S(1)} %get-tuple-element.11, f32[1536]{0:T(1024)S(1)} %get-tuple-element.10), kind=kOutput, calls=%fused_computation.25 | convolution fusion | flops 170477568 | bytes 2703648 | tf_op jit(solution)/shard_map/dot_general | solution.py:47
  126.8 32.5 %all-gather.9.cloned.1.call-done = bf16[1152,768]{1,0:T(8,128)(2,1)} async-done(((bf16[72,768]{1,0:T(8,128)(2,1)}), bf16[1152,768]{1,0:T(8,128)(2,1)}) %all-gather.9.cloned.1.call-update) | async-done | bytes 1769488 | tf_op jit(solution)/shard_map/all_gather | solution.py:54
  159.3 3.9 %copy.22 = bf16[1152,768]{0,1:T(8,128)(2,1)} copy(bf16[1152,768]{1,0:T(8,128)(2,1)} %all-gather.9.cloned.1.call-done) | data formatting | bytes 3538944 | tf_op jit(solution)/shard_map/all_gather | solution.py:54
  163.1 2.1 fusion.60
  165.2 0.0 copy-start.1
  165.2 1.3 copy-done.1
  166.5 0.5 fusion.4
  167.0 34.0 %all-gather.11.cloned.1.call-done = bf16[1152,768]{1,0:T(8,128)(2,1)} async-done(((bf16[72,768]{1,0:T(8,128)(2,1)}), bf16[1152,768]{1,0:T(8,128)(2,1)}) %all-gather.11.cloned.1.call-update) | async-done | bytes 1769488 | tf_op jit(solution)/shard_map/all_gather | solution.py:55
  201.0 3.9 %copy.25 = bf16[1152,768]{0,1:T(8,128)(2,1)} copy(bf16[1152,768]{1,0:T(8,128)(2,1)} %all-gather.11.cloned.1.call-done) | data formatting | bytes 3538944 | tf_op jit(solution)/shard_map/all_gather | solution.py:55
  204.8 3.0 %fusion.10 = bf16[6,9,8,128]{3,2,1,0:T(8,128)(2,1)S(1)} fusion(bf16[1152,6,128]{0,2,1:T(8,128)(2,1)} %bitcast.75, f32[6,72,1152]{2,1,0:T(8,128)} %copy-done.1, f32[6,72]{1,0:T(8,128)S(1)} %broadcast_maximum_fusion, pred[1152]{0:T(1024)(128)(4,1)S(1)} %fusion.43, f32[72,6]{0,1:T(8,128)S(1)} %bitcast.79), kind=kOutput, calls=%fused_computation.22 | convolution fusion | flops 129005568 | bytes 3875328 | tf_op jit(solution)/shard_map/hrp,phd->hrd/dot_general | solution.py:71
  207.8 0.5 convert_bitcast_fusion
  208.4 0.8 pad_maximum_fusion.1
  209.2 0.8 pad_maximum_fusion
  (8 shorter events, 0.1 us)
Async XLA Ops:
  7.2 100.2 %copy-start = (bf16[768,1536]{1,0:T(8,128)(2,1)S(1)}, bf16[768,1536]{1,0:T(8,128)(2,1)}, u32[]{:S(2)}) copy-start(bf16[768,1536]{1,0:T(8,128)(2,1)} %param.15) | copy-start | bytes 7077892
  7.2 5.5 %copy-start.3 = (bf16[72,1536]{1,0:T(8,128)(2,1)S(1)}, bf16[72,1536]{1,0:T(8,128)(2,1)}, u32[]{:S(2)}) copy-start(bf16[72,1536]{1,0:T(8,128)(2,1)} %param.8) | copy-start | bytes 663556
  7.2 51.5 %all-gather.5.cloned.1.call-start = ((), (), s32[]{:S(2)}) async-start(), calls=%async_computation | async-start | bytes 1880064 | tf_op jit(solution)/shard_map/all_gather | solution.py:54
  15.6 85.0 %all-gather.7.cloned.1.call-start = ((), (), s32[]{:S(2)}) async-start(), calls=%async_computation.1 | async-start | bytes 1880064 | tf_op jit(solution)/shard_map/all_gather | solution.py:55
  18.5 140.8 %all-gather.9.cloned.1.call-start = ((), (), s32[]{:S(2)}) async-start(), calls=%async_computation.2 | async-start | bytes 1880064 | tf_op jit(solution)/shard_map/all_gather | solution.py:54
  64.6 1.3 copy-start.2
  107.4 10.1 %copy-start.4 = (bf16[72,1536]{1,0:T(8,128)(2,1)S(1)}, bf16[72,1536]{1,0:T(8,128)(2,1)}, u32[]{:S(2)}) copy-start(bf16[72,1536]{1,0:T(8,128)(2,1)} %param.9) | copy-start | bytes 663556
  108.0 9.6 %collective-permute-start = (bf16[72,1536]{1,0:T(8,128)(2,1)S(1)}, bf16[72,1536]{1,0:T(8,128)(2,1)}, u32[]{:S(2)}, u32[]{:S(2)}) collective-permute-start(bf16[72,1536]{1,0:T(8,128)(2,1)S(1)} %get-tuple-element.7), channel_id=1, source_target_pairs={{4,0},{5,1},{6,2},{7,3},{8,4},{9,5},{10,6},{11,7},{12,8},{13,9},{1... | collective-permute-start | bytes 663560 | tf_op jit(solution)/shard_map/ppermute | solution.py:18
  121.6 79.4 %all-gather.11.cloned.1.call-start = ((), (), s32[]{:S(2)}) async-start(), calls=%async_computation.3 | async-start | bytes 1880064 | tf_op jit(solution)/shard_map/all_gather | solution.py:55
  165.2 1.3 copy-start.1
Sparse Core Ops, SparseCore 0:
  15.7 42.9 all-gather.4
  61.4 39.0 all-gather.6
  121.7 37.5 all-gather.8
  161.9 39.0 all-gather.10
where the time goes:
time: 217 us
  waiting for transfers between devices  146 us (67%)
  matrix products  29.4 us (14%)
  local copies, waits for them, and re-layouts  18 us (8%)
  between operations  15.6 us (7%)
  other arithmetic  6.41 us (3%)
    all_gather x2, waiting for transfers between devices, denoise_local(): lax.all_gather(local_keys, 'tok', axis=0, tiled=True)  69.2 us
    all_gather x2, waiting for transfers between devices, denoise_local(): lax.all_gather(local_values, 'tok', axis=0, tiled=True)  68.1 us
    ppermute x1, waiting for transfers between devices, shifted(): return lax.ppermute(block, axis, route)  8.25 us
    all_gather x2, local copies, waits for them, and re-layouts, denoise_local(): lax.all_gather(local_keys, 'tok', axis=0, tiled=True)  7.7 us
    all_gather x2, local copies, waits for them, and re-layouts, denoise_local(): lax.all_gather(local_values, 'tok', axis=0, tiled=True)  7.7 us
    dot_general x2, matrix products, denoise_local(): jnp.einsum('hrp,phd->hrd', weights.astype(jnp.bfloat16), gathered_values....  5.99 us
    dot_general x2, matrix products, denoise_local(): jnp.dot(hidden, w_key, preferred_element_type=jnp.float32)  5.8 us
    dot_general x2, matrix products, denoise_local(): jnp.dot(hidden, w_value, preferred_element_type=jnp.float32)  5.79 us
  transfers between devices with their start and end apart: 5, of which 5 were waited for; matrix products, arithmetic and copies ran while one was open for 11% of the time, Pallas kernels for 0%

commit v1 on v0

--- a/solution.py
+++ b/solution.py
@@ -10,6 +10,27 @@
 TFREQ = 256
 SECTIONS = 4
 epsilon = 1e-06
+
+
+def gather_around(x, axis, dim):
+    devices, index, width = (lax.axis_size(axis), lax.axis_index(axis), x.shape[dim])
+    upward = [(i, (i + 1) % devices) for i in range(devices)]
+    downward = [(i, (i - 1) % devices) for i in range(devices)]
+    whole = jnp.zeros((*x.shape[:dim], devices * width, *x.shape[dim + 1 :]), x.dtype)
+    whole = lax.dynamic_update_slice_in_dim(whole, x, index * width, axis=dim)
+    from_left = from_right = x
+    half = devices // 2
+    for step in range(1, half + 1):
+        from_left = lax.ppermute(from_left, axis, upward)
+        whole = lax.dynamic_update_slice_in_dim(
+            whole, from_left, (index - step) % devices * width, axis=dim
+        )
+        if step < devices - half:
+            from_right = lax.ppermute(from_right, axis, downward)
+            whole = lax.dynamic_update_slice_in_dim(
+                whole, from_right, (index + step) % devices * width, axis=dim
+            )
+    return whole
 
 
 def shifted(block, axis, distance):
@@ -51,7 +72,7 @@
             jnp.bfloat16
         )
         gathered_keys, gathered_values = (
-            lax.all_gather(local_keys, "tok", axis=0, tiled=True),
+            gather_around(local_keys, "tok", 0),
             lax.all_gather(local_values, "tok", axis=0, tiled=True),
         )
         best = jnp.full((HEADS, local_rows), -1e30, jnp.float32)

time: 217 us -> 313 us (1.44); the launches traced: 217 us -> 308 us
  local copies, waits for them, and re-layouts: 18 us -> 152 us
  waiting for transfers between devices: 146 us -> 42.9 us
  starting transfers between devices: 1.45 us -> 65.5 us
  matrix products: 29.4 us -> 25.6 us
    dynamic_update_slice x0 -> x32, local copies, waits for them, and re-layouts: none -> 118 us  [the longest x16 58.8 us: gather_around(): lax.dynamic_update_slice_in_dim(whole, from_left, (index - step) % device...]
    all_gather x2 -> x0, waiting for transfers between devices: 69.2 us -> none  [denoise_local(): lax.all_gather(local_keys, 'tok', axis=0, tiled=True)]
    all_gather x2, waiting for transfers between devices: 68.1 us -> 0.04 us  [denoise_local(): lax.all_gather(local_values, 'tok', axis=0, tiled=True)]
    ppermute x0 -> x30, starting transfers between devices: none -> 64.2 us  [the longest x14 63.2 us: gather_around(): from_right = lax.ppermute(from_right, axis, downward)]
    ppermute x0 -> x30, waiting for transfers between devices: none -> 36.3 us  [the longest x16 34.4 us: gather_around(): from_left = lax.ppermute(from_left, axis, upward)]
    ppermute x0 -> x30, local copies, waits for them, and re-layouts: none -> 20.1 us  [the longest x16 11.6 us: gather_around(): from_left = lax.ppermute(from_left, axis, upward)]
    all_gather x2 -> x0, local copies, waits for them, and re-layouts: 7.7 us -> none  [denoise_local(): lax.all_gather(local_keys, 'tok', axis=0, tiled=True)]
  transfers between devices with their start and end apart: 5 -> 33, of which waited for: 5 -> 15; matrix products, arithmetic and copies ran while one was open for 11% -> 50% of each run, Pallas kernels for 0% -> 0%
where the time goes in v1:
time: 313 us; the launch traced here: 308 us
  local copies, waits for them, and re-layouts  152 us (49%)
  starting transfers between devices  65.5 us (21%)
  waiting for transfers between devices  42.9 us (14%)
  matrix products  25.6 us (8%)
  between operations  16.9 us (5%)
  other arithmetic  5.52 us (2%)
    ppermute x14, starting transfers between devices, gather_around(): from_right = lax.ppermute(from_right, axis, downward)  63.2 us
    dynamic_update_slice x16, local copies, waits for them, and re-layouts, gather_around(): lax.dynamic_update_slice_in_dim(whole, from_left, (index - step) % device...  58.8 us
    dynamic_update_slice x14, local copies, waits for them, and re-layouts, gather_around(): lax.dynamic_update_slice_in_dim(whole, from_right, (index + step) % devic...  52.5 us
    ppermute x16, waiting for transfers between devices, gather_around(): from_left = lax.ppermute(from_left, axis, upward)  34.4 us
    ppermute x16, local copies, waits for them, and re-layouts, gather_around(): from_left = lax.ppermute(from_left, axis, upward)  11.6 us
    ppermute x14, local copies, waits for them, and re-layouts, gather_around(): from_right = lax.ppermute(from_right, axis, downward)  8.55 us
    all_gather x2, local copies, waits for them, and re-layouts, denoise_local(): lax.all_gather(local_values, 'tok', axis=0, tiled=True)  7.72 us
    dynamic_update_slice x2, local copies, waits for them, and re-layouts, gather_around(): whole = lax.dynamic_update_slice_in_dim(whole, x, index * width, axis=dim)  6.69 us
  transfers between devices with their start and end apart: 33, of which 15 were waited for; matrix products, arithmetic and copies ran while one was open for 50% of the time, Pallas kernels for 0%

profile of v1, /device:TPU:0, one launch (start us, length us, event | category | flops | bytes accessed | tf_op | source)
XLA Modules:
  0.0 308.2 jit_solution(14825002290798596016)
XLA Ops:
  12.8 2.9 convolution_convert_fusion.3
  15.7 2.4 convolution_convert_fusion.4
  18.7 5.0 %collective-permute-start.1 = (bf16[72,768]{1,0:T(8,128)(2,1)S(1)}, bf16[72,768]{1,0:T(8,128)(2,1)S(1)}, u32[]{:S(2)}, u32[]{:S(2)}) collective-permute-start(bf16[72,768]{1,0:T(8,128)(2,1)S(1)} %convolution_convert_fusion.4), channel_id=1, source_target_pairs={{0,15},{1,0},{2,1},{3,2},{4,3},{5,4},{6,5},{7,6},{8,7},{9,8},{10,9... | collective-permute-start | bytes 331784 | tf_op jit(solution)/shard_map/ppermute | solution.py:29
  23.7 2.5 collective-permute-done
  26.2 4.4 %collective-permute-start.3 = (bf16[72,768]{1,0:T(8,128)(2,1)S(1)}, bf16[72,768]{1,0:T(8,128)(2,1)S(1)}, u32[]{:S(2)}, u32[]{:S(2)}) collective-permute-start(bf16[72,768]{1,0:T(8,128)(2,1)S(1)} %collective-permute-done.1), channel_id=1, source_target_pairs={{0,15},{1,0},{2,1},{3,2},{4,3},{5,4},{6,5},{7,6},{8,7},{9,8},{10,9... | collective-permute-start | bytes 331784 | tf_op jit(solution)/shard_map/ppermute | solution.py:29
  30.6 3.9 %collective-permute-done.2 = bf16[72,768]{1,0:T(8,128)(2,1)S(1)} collective-permute-done((bf16[72,768]{1,0:T(8,128)(2,1)S(1)}, bf16[72,768]{1,0:T(8,128)(2,1)S(1)}, u32[]{:S(2)}, u32[]{:S(2)}) %collective-permute-start.2) | collective-permute-done | bytes 110624 | tf_op jit(solution)/shard_map/ppermute | solution.py:24
  34.5 4.4 %collective-permute-start.5 = (bf16[72,768]{1,0:T(8,128)(2,1)S(1)}, bf16[72,768]{1,0:T(8,128)(2,1)S(1)}, u32[]{:S(2)}, u32[]{:S(2)}) collective-permute-start(bf16[72,768]{1,0:T(8,128)(2,1)S(1)} %collective-permute-done.3), channel_id=1, source_target_pairs={{0,15},{1,0},{2,1},{3,2},{4,3},{5,4},{6,5},{7,6},{8,7},{9,8},{10,9... | collective-permute-start | bytes 331784 | tf_op jit(solution)/shard_map/ppermute | solution.py:29
  38.9 2.5 collective-permute-done.4
  41.5 4.4 %collective-permute-start.7 = (bf16[72,768]{1,0:T(8,128)(2,1)S(1)}, bf16[72,768]{1,0:T(8,128)(2,1)S(1)}, u32[]{:S(2)}, u32[]{:S(2)}) collective-permute-start(bf16[72,768]{1,0:T(8,128)(2,1)S(1)} %collective-permute-done.5), channel_id=1, source_target_pairs={{0,15},{1,0},{2,1},{3,2},{4,3},{5,4},{6,5},{7,6},{8,7},{9,8},{10,9... | collective-permute-start | bytes 331784 | tf_op jit(solution)/shard_map/ppermute | solution.py:29
  45.9 2.5 collective-permute-done.6
  48.5 4.6 %collective-permute-start.9 = (bf16[72,768]{1,0:T(8,128)(2,1)S(1)}, bf16[72,768]{1,0:T(8,128)(2,1)}, u32[]{:S(2)}, u32[]{:S(2)}) collective-permute-start(bf16[72,768]{1,0:T(8,128)(2,1)S(1)} %collective-permute-done.7), channel_id=1, source_target_pairs={{0,15},{1,0},{2,1},{3,2},{4,3},{5,4},{6,5},{7,6},{8,7},{9,8},{10,9... | collective-permute-start | bytes 331784 | tf_op jit(solution)/shard_map/ppermute | solution.py:29
  57.3 4.7 %collective-permute-start.11 = (bf16[72,768]{1,0:T(8,128)(2,1)}, bf16[72,768]{1,0:T(8,128)(2,1)}, u32[]{:S(2)}, u32[]{:S(2)}) collective-permute-start(bf16[72,768]{1,0:T(8,128)(2,1)} %collective-permute-done.9), channel_id=1, source_target_pairs={{0,15},{1,0},{2,1},{3,2},{4,3},{5,4},{6,5},{7,6},{8,7},{9,8},{10,9... | collective-permute-start | bytes 331784 | tf_op jit(solution)/shard_map/ppermute | solution.py:29
  66.4 3.4 %dynamic_update_slice.96 = bf16[1152,768]{0,1:T(8,128)(2,1)} dynamic-update-slice(bf16[1152,768]{0,1:T(8,128)(2,1)} %broadcast.105.clone, bf16[72,768]{0,1:T(8,128)(2,1)S(1)} %copy.14, s32[]{:T(128)S(6)} %select_n.203, s32[]{:T(128)} %constant.159.clone.1) | dynamic-update-slice | bytes 221188 | tf_op jit(solution)/shard_map/dynamic_update_slice | solution.py:20
  69.7 4.2 %collective-permute-start.13 = (bf16[72,768]{1,0:T(8,128)(2,1)}, bf16[72,768]{1,0:T(8,128)(2,1)}, u32[]{:S(2)}, u32[]{:S(2)}) collective-permute-start(bf16[72,768]{1,0:T(8,128)(2,1)} %collective-permute-done.11), channel_id=1, source_target_pairs={{0,15},{1,0},{2,1},{3,2},{4,3},{5,4},{6,5},{7,6},{8,7},{9,8},{10,9... | collective-permute-start | bytes 331784 | tf_op jit(solution)/shard_map/ppermute | solution.py:29
  74.1 3.2 %dynamic_update_slice.97 = bf16[1152,768]{0,1:T(8,128)(2,1)} dynamic-update-slice(bf16[1152,768]{0,1:T(8,128)(2,1)} %dynamic_update_slice.96, bf16[72,768]{0,1:T(8,128)(2,1)S(1)} %copy.15, s32[]{:T(128)S(6)} %select_n.205, s32[]{:T(128)} %constant.159.clone.1) | dynamic-update-slice | bytes 221188 | tf_op jit(solution)/shard_map/dynamic_update_slice | solution.py:25
  77.5 3.8 %dynamic_update_slice.98 = bf16[1152,768]{0,1:T(8,128)(2,1)} dynamic-update-slice(bf16[1152,768]{0,1:T(8,128)(2,1)} %dynamic_update_slice.97, bf16[72,768]{0,1:T(8,128)(2,1)S(1)} %copy.16, s32[]{:T(128)S(6)} %select_n.207, s32[]{:T(128)} %constant.159.clone.1) | dynamic-update-slice | bytes 221188 | tf_op jit(solution)/shard_map/dynamic_update_slice | solution.py:30
  81.5 3.8 %dynamic_update_slice.99 = bf16[1152,768]{0,1:T(8,128)(2,1)} dynamic-update-slice(bf16[1152,768]{0,1:T(8,128)(2,1)} %dynamic_update_slice.98, bf16[72,768]{0,1:T(8,128)(2,1)S(1)} %copy.17, s32[]{:T(128)S(6)} %select_n.209, s32[]{:T(128)} %constant.159.clone.1) | dynamic-update-slice | bytes 221188 | tf_op jit(solution)/shard_map/dynamic_update_slice | solution.py:25
  85.4 3.8 %dynamic_update_slice.100 = bf16[1152,768]{0,1:T(8,128)(2,1)} dynamic-update-slice(bf16[1152,768]{0,1:T(8,128)(2,1)} %dynamic_update_slice.99, bf16[72,768]{0,1:T(8,128)(2,1)S(1)} %copy.18, s32[]{:T(128)S(6)} %select_n.211, s32[]{:T(128)} %constant.159.clone.1) | dynamic-update-slice | bytes 221188 | tf_op jit(solution)/shard_map/dynamic_update_slice | solution.py:30
  89.4 3.8 %dynamic_update_slice.101 = bf16[1152,768]{0,1:T(8,128)(2,1)} dynamic-update-slice(bf16[1152,768]{0,1:T(8,128)(2,1)} %dynamic_update_slice.100, bf16[72,768]{0,1:T(8,128)(2,1)S(1)} %copy.19, s32[]{:T(128)S(6)} %select_n.213, s32[]{:T(128)} %constant.159.clone.1) | dynamic-update-slice | bytes 221188 | tf_op jit(solution)/shard_map/dynamic_update_slice | solution.py:25
  93.3 3.8 %dynamic_update_slice.102 = bf16[1152,768]{0,1:T(8,128)(2,1)} dynamic-update-slice(bf16[1152,768]{0,1:T(8,128)(2,1)} %dynamic_update_slice.101, bf16[72,768]{0,1:T(8,128)(2,1)S(1)} %copy.20, s32[]{:T(128)S(6)} %select_n.215, s32[]{:T(128)} %constant.159.clone.1) | dynamic-update-slice | bytes 221188 | tf_op jit(solution)/shard_map/dynamic_update_slice | solution.py:30
  97.2 3.7 %dynamic_update_slice.103 = bf16[1152,768]{0,1:T(8,128)(2,1)} dynamic-update-slice(bf16[1152,768]{0,1:T(8,128)(2,1)} %dynamic_update_slice.102, bf16[72,768]{0,1:T(8,128)(2,1)S(1)} %copy.21, s32[]{:T(128)S(6)} %select_n.217, s32[]{:T(128)} %constant.159.clone.1) | dynamic-update-slice | bytes 221188 | tf_op jit(solution)/shard_map/dynamic_update_slice | solution.py:25
  101.1 3.7 %dynamic_update_slice.104 = bf16[1152,768]{0,1:T(8,128)(2,1)} dynamic-update-slice(bf16[1152,768]{0,1:T(8,128)(2,1)} %dynamic_update_slice.103, bf16[72,768]{0,1:T(8,128)(2,1)S(1)} %copy.22, s32[]{:T(128)S(6)} %select_n.219, s32[]{:T(128)} %constant.159.clone.1) | dynamic-update-slice | bytes 221188 | tf_op jit(solution)/shard_map/dynamic_update_slice | solution.py:30
  105.0 3.7 %dynamic_update_slice.105 = bf16[1152,768]{0,1:T(8,128)(2,1)} dynamic-update-slice(bf16[1152,768]{0,1:T(8,128)(2,1)} %dynamic_update_slice.104, bf16[72,768]{0,1:T(8,128)(2,1)S(1)} %copy.23, s32[]{:T(128)S(6)} %select_n.221, s32[]{:T(128)} %constant.159.clone.1) | dynamic-update-slice | bytes 221188 | tf_op jit(solution)/shard_map/dynamic_update_slice | solution.py:25
  109.8 3.7 %dynamic_update_slice.106 = bf16[1152,768]{0,1:T(8,128)(2,1)} dynamic-update-slice(bf16[1152,768]{0,1:T(8,128)(2,1)} %dynamic_update_slice.105, bf16[72,768]{0,1:T(8,128)(2,1)S(1)} %copy.24, s32[]{:T(128)S(6)} %select_n.223, s32[]{:T(128)} %constant.159.clone.1) | dynamic-update-slice | bytes 221188 | tf_op jit(solution)/shard_map/dynamic_update_slice | solution.py:30
  114.6 3.7 %dynamic_update_slice.107 = bf16[1152,768]{0,1:T(8,128)(2,1)} dynamic-update-slice(bf16[1152,768]{0,1:T(8,128)(2,1)} %dynamic_update_slice.106, bf16[72,768]{0,1:T(8,128)(2,1)S(1)} %copy.25, s32[]{:T(128)S(6)} %select_n.225, s32[]{:T(128)} %constant.159.clone.1) | dynamic-update-slice | bytes 221188 | tf_op jit(solution)/shard_map/dynamic_update_slice | solution.py:25
  119.4 3.7 %dynamic_update_slice.108 = bf16[1152,768]{0,1:T(8,128)(2,1)} dynamic-update-slice(bf16[1152,768]{0,1:T(8,128)(2,1)} %dynamic_update_slice.107, bf16[72,768]{0,1:T(8,128)(2,1)S(1)} %copy.26, s32[]{:T(128)S(6)} %select_n.227, s32[]{:T(128)} %constant.159.clone.1) | dynamic-update-slice | bytes 221188 | tf_op jit(solution)/shard_map/dynamic_update_slice | solution.py:30
  124.2 3.7 %dynamic_update_slice.109 = bf16[1152,768]{0,1:T(8,128)(2,1)} dynamic-update-slice(bf16[1152,768]{0,1:T(8,128)(2,1)} %dynamic_update_slice.108, bf16[72,768]{0,1:T(8,128)(2,1)S(1)} %copy.27, s32[]{:T(128)S(6)} %select_n.229, s32[]{:T(128)} %constant.159.clone.1) | dynamic-update-slice | bytes 221188 | tf_op jit(solution)/shard_map/dynamic_update_slice | solution.py:25
  129.1 3.7 %dynamic_update_slice.110 = bf16[1152,768]{0,1:T(8,128)(2,1)} dynamic-update-slice(bf16[1152,768]{0,1:T(8,128)(2,1)} %dynamic_update_slice.109, bf16[72,768]{0,1:T(8,128)(2,1)S(1)} %copy.28, s32[]{:T(128)S(6)} %select_n.231, s32[]{:T(128)} %constant.159.clone.1) | dynamic-update-slice | bytes 221188 | tf_op jit(solution)/shard_map/dynamic_update_slice | solution.py:30
  133.9 3.7 %dynamic_update_slice.111 = bf16[1152,768]{0,1:T(8,128)(2,1)} dynamic-update-slice(bf16[1152,768]{0,1:T(8,128)(2,1)} %dynamic_update_slice.110, bf16[72,768]{0,1:T(8,128)(2,1)S(1)} %copy.29, s32[]{:T(128)S(6)} %select_n.233, s32[]{:T(128)} %constant.159.clone.1) | dynamic-update-slice | bytes 221188 | tf_op jit(solution)/shard_map/dynamic_update_slice | solution.py:25
  141.5 3.9 %copy.32 = bf16[1152,768]{0,1:T(8,128)(2,1)} copy(bf16[1152,768]{1,0:T(8,128)(2,1)} %all-gather.3.cloned.1.call-done) | data formatting | bytes 3538944 | tf_op jit(solution)/shard_map/all_gather | solution.py:76
  145.4 3.0 fusion.11
  150.3 6.5 %collective-permute-done.15 = bf16[72,1536]{1,0:T(8,128)(2,1)S(1)} collective-permute-done((bf16[72,1536]{1,0:T(8,128)(2,1)S(1)}, bf16[72,1536]{1,0:T(8,128)(2,1)S(1)}, u32[]{:S(2)}, u32[]{:S(2)}) %collective-permute-start.15) | collective-permute-done | bytes 221216 | tf_op jit(solution)/shard_map/ppermute | solution.py:39
  157.0 2.9 convolution_convert_fusion
  162.4 4.4 %collective-permute-start.17 = (bf16[72,768]{1,0:T(8,128)(2,1)S(1)}, bf16[72,768]{1,0:T(8,128)(2,1)S(1)}, u32[]{:S(2)}, u32[]{:S(2)}) collective-permute-start(bf16[72,768]{1,0:T(8,128)(2,1)S(1)} %convolution_convert_fusion.1), channel_id=1, source_target_pairs={{0,15},{1,0},{2,1},{3,2},{4,3},{5,4},{6,5},{7,6},{8,7},{9,8},{10,9... | collective-permute-start | bytes 331784 | tf_op jit(solution)/shard_map/ppermute | solution.py:29
  166.8 2.5 collective-permute-done.16
  169.4 4.5 %collective-permute-start.19 = (bf16[72,768]{1,0:T(8,128)(2,1)S(1)}, bf16[72,768]{1,0:T(8,128)(2,1)S(1)}, u32[]{:S(2)}, u32[]{:S(2)}) collective-permute-start(bf16[72,768]{1,0:T(8,128)(2,1)S(1)} %collective-permute-done.17), channel_id=1, source_target_pairs={{0,15},{1,0},{2,1},{3,2},{4,3},{5,4},{6,5},{7,6},{8,7},{9,8},{10,9... | collective-permute-start | bytes 331784 | tf_op jit(solution)/shard_map/ppermute | solution.py:29
  173.9 2.7 collective-permute-done.18
  176.6 4.5 %collective-permute-start.21 = (bf16[72,768]{1,0:T(8,128)(2,1)S(1)}, bf16[72,768]{1,0:T(8,128)(2,1)S(1)}, u32[]{:S(2)}, u32[]{:S(2)}) collective-permute-start(bf16[72,768]{1,0:T(8,128)(2,1)S(1)} %collective-permute-done.19), channel_id=1, source_target_pairs={{0,15},{1,0},{2,1},{3,2},{4,3},{5,4},{6,5},{7,6},{8,7},{9,8},{10,9... | collective-permute-start | bytes 331784 | tf_op jit(solution)/shard_map/ppermute | solution.py:29
  181.1 2.4 collective-permute-done.20
  183.6 4.5 %collective-permute-start.23 = (bf16[72,768]{1,0:T(8,128)(2,1)S(1)}, bf16[72,768]{1,0:T(8,128)(2,1)S(1)}, u32[]{:S(2)}, u32[]{:S(2)}) collective-permute-start(bf16[72,768]{1,0:T(8,128)(2,1)S(1)} %collective-permute-done.21), channel_id=1, source_target_pairs={{0,15},{1,0},{2,1},{3,2},{4,3},{5,4},{6,5},{7,6},{8,7},{9,8},{10,9... | collective-permute-start | bytes 331784 | tf_op jit(solution)/shard_map/ppermute | solution.py:29
  188.1 4.6 %collective-permute-done.22 = bf16[72,768]{1,0:T(8,128)(2,1)S(1)} collective-permute-done((bf16[72,768]{1,0:T(8,128)(2,1)S(1)}, bf16[72,768]{1,0:T(8,128)(2,1)S(1)}, u32[]{:S(2)}, u32[]{:S(2)}) %collective-permute-start.22) | collective-permute-done | bytes 110624 | tf_op jit(solution)/shard_map/ppermute | solution.py:24
  192.7 4.4 %collective-permute-start.25 = (bf16[72,768]{1,0:T(8,128)(2,1)S(1)}, bf16[72,768]{1,0:T(8,128)(2,1)S(1)}, u32[]{:S(2)}, u32[]{:S(2)}) collective-permute-start(bf16[72,768]{1,0:T(8,128)(2,1)S(1)} %collective-permute-done.23), channel_id=1, source_target_pairs={{0,15},{1,0},{2,1},{3,2},{4,3},{5,4},{6,5},{7,6},{8,7},{9,8},{10,9... | collective-permute-start | bytes 331784 | tf_op jit(solution)/shard_map/ppermute | solution.py:29
  197.1 3.0 collective-permute-done.24
  200.1 4.4 %collective-permute-start.27 = (bf16[72,768]{1,0:T(8,128)(2,1)S(1)}, bf16[72,768]{1,0:T(8,128)(2,1)}, u32[]{:S(2)}, u32[]{:S(2)}) collective-permute-start(bf16[72,768]{1,0:T(8,128)(2,1)S(1)} %collective-permute-done.25), channel_id=1, source_target_pairs={{0,15},{1,0},{2,1},{3,2},{4,3},{5,4},{6,5},{7,6},{8,7},{9,8},{10,9... | collective-permute-start | bytes 331784 | tf_op jit(solution)/shard_map/ppermute | solution.py:29
  204.6 2.5 collective-permute-done.26
  207.1 4.5 %collective-permute-start.29 = (bf16[72,768]{1,0:T(8,128)(2,1)}, bf16[72,768]{1,0:T(8,128)(2,1)}, u32[]{:S(2)}, u32[]{:S(2)}) collective-permute-start(bf16[72,768]{1,0:T(8,128)(2,1)} %collective-permute-done.27), channel_id=1, source_target_pairs={{0,15},{1,0},{2,1},{3,2},{4,3},{5,4},{6,5},{7,6},{8,7},{9,8},{10,9... | collective-permute-start | bytes 331784 | tf_op jit(solution)/shard_map/ppermute | solution.py:29
  217.1 3.3 %dynamic_update_slice.112 = bf16[1152,768]{0,1:T(8,128)(2,1)} dynamic-update-slice(bf16[1152,768]{0,1:T(8,128)(2,1)} %broadcast.105, bf16[72,768]{0,1:T(8,128)(2,1)S(1)} %copy.35, s32[]{:T(128)S(6)} %select_n.203, s32[]{:T(128)} %constant.159.clone.1) | dynamic-update-slice | bytes 221188 | tf_op jit(solution)/shard_map/dynamic_update_slice | solution.py:20
  221.5 3.1 %dynamic_update_slice.113 = bf16[1152,768]{0,1:T(8,128)(2,1)} dynamic-update-slice(bf16[1152,768]{0,1:T(8,128)(2,1)} %dynamic_update_slice.112, bf16[72,768]{0,1:T(8,128)(2,1)S(1)} %copy.36, s32[]{:T(128)S(6)} %select_n.205, s32[]{:T(128)} %constant.159.clone.1) | dynamic-update-slice | bytes 221188 | tf_op jit(solution)/shard_map/dynamic_update_slice | solution.py:25
  224.8 3.8 %dynamic_update_slice.114 = bf16[1152,768]{0,1:T(8,128)(2,1)} dynamic-update-slice(bf16[1152,768]{0,1:T(8,128)(2,1)} %dynamic_update_slice.113, bf16[72,768]{0,1:T(8,128)(2,1)S(1)} %copy.37, s32[]{:T(128)S(6)} %select_n.207, s32[]{:T(128)} %constant.159.clone.1) | dynamic-update-slice | bytes 221188 | tf_op jit(solution)/shard_map/dynamic_update_slice | solution.py:30
  229.7 3.8 %dynamic_update_slice.115 = bf16[1152,768]{0,1:T(8,128)(2,1)} dynamic-update-slice(bf16[1152,768]{0,1:T(8,128)(2,1)} %dynamic_update_slice.114, bf16[72,768]{0,1:T(8,128)(2,1)S(1)} %copy.38, s32[]{:T(128)S(6)} %select_n.209, s32[]{:T(128)} %constant.159.clone.1) | dynamic-update-slice | bytes 221188 | tf_op jit(solution)/shard_map/dynamic_update_slice | solution.py:25
  234.5 3.8 %dynamic_update_slice.116 = bf16[1152,768]{0,1:T(8,128)(2,1)} dynamic-update-slice(bf16[1152,768]{0,1:T(8,128)(2,1)} %dynamic_update_slice.115, bf16[72,768]{0,1:T(8,128)(2,1)S(1)} %copy.39, s32[]{:T(128)S(6)} %select_n.211, s32[]{:T(128)} %constant.159.clone.1) | dynamic-update-slice | bytes 221188 | tf_op jit(solution)/shard_map/dynamic_update_slice | solution.py:30
  239.3 3.8 %dynamic_update_slice.117 = bf16[1152,768]{0,1:T(8,128)(2,1)} dynamic-update-slice(bf16[1152,768]{0,1:T(8,128)(2,1)} %dynamic_update_slice.116, bf16[72,768]{0,1:T(8,128)(2,1)S(1)} %copy.40, s32[]{:T(128)S(6)} %select_n.213, s32[]{:T(128)} %constant.159.clone.1) | dynamic-update-slice | bytes 221188 | tf_op jit(solution)/shard_map/dynamic_update_slice | solution.py:25
  243.2 3.8 %dynamic_update_slice.118 = bf16[1152,768]{0,1:T(8,128)(2,1)} dynamic-update-slice(bf16[1152,768]{0,1:T(8,128)(2,1)} %dynamic_update_slice.117, bf16[72,768]{0,1:T(8,128)(2,1)S(1)} %copy.41, s32[]{:T(128)S(6)} %select_n.215, s32[]{:T(128)} %constant.159.clone.1) | dynamic-update-slice | bytes 221188 | tf_op jit(solution)/shard_map/dynamic_update_slice | solution.py:30
  248.1 3.7 %dynamic_update_slice.119 = bf16[1152,768]{0,1:T(8,128)(2,1)} dynamic-update-slice(bf16[1152,768]{0,1:T(8,128)(2,1)} %dynamic_update_slice.118, bf16[72,768]{0,1:T(8,128)(2,1)S(1)} %copy.42, s32[]{:T(128)S(6)} %select_n.217, s32[]{:T(128)} %constant.159.clone.1) | dynamic-update-slice | bytes 221188 | tf_op jit(solution)/shard_map/dynamic_update_slice | solution.py:25
  252.9 3.7 %dynamic_update_slice.120 = bf16[1152,768]{0,1:T(8,128)(2,1)} dynamic-update-slice(bf16[1152,768]{0,1:T(8,128)(2,1)} %dynamic_update_slice.119, bf16[72,768]{0,1:T(8,128)(2,1)S(1)} %copy.43, s32[]{:T(128)S(6)} %select_n.219, s32[]{:T(128)} %constant.159.clone.1) | dynamic-update-slice | bytes 221188 | tf_op jit(solution)/shard_map/dynamic_update_slice | solution.py:30
  257.7 3.7 %dynamic_update_slice.121 = bf16[1152,768]{0,1:T(8,128)(2,1)} dynamic-update-slice(bf16[1152,768]{0,1:T(8,128)(2,1)} %dynamic_update_slice.120, bf16[72,768]{0,1:T(8,128)(2,1)S(1)} %copy.44, s32[]{:T(128)S(6)} %select_n.221, s32[]{:T(128)} %constant.159.clone.1) | dynamic-update-slice | bytes 221188 | tf_op jit(solution)/shard_map/dynamic_update_slice | solution.py:25
  261.6 3.7 %dynamic_update_slice.122 = bf16[1152,768]{0,1:T(8,128)(2,1)} dynamic-update-slice(bf16[1152,768]{0,1:T(8,128)(2,1)} %dynamic_update_slice.121, bf16[72,768]{0,1:T(8,128)(2,1)S(1)} %copy.45, s32[]{:T(128)S(6)} %select_n.223, s32[]{:T(128)} %constant.159.clone.1) | dynamic-update-slice | bytes 221188 | tf_op jit(solution)/shard_map/dynamic_update_slice | solution.py:30
  266.4 3.7 %dynamic_update_slice.123 = bf16[1152,768]{0,1:T(8,128)(2,1)} dynamic-update-slice(bf16[1152,768]{0,1:T(8,128)(2,1)} %dynamic_update_slice.122, bf16[72,768]{0,1:T(8,128)(2,1)S(1)} %copy.46, s32[]{:T(128)S(6)} %select_n.225, s32[]{:T(128)} %constant.159.clone.1) | dynamic-update-slice | bytes 221188 | tf_op jit(solution)/shard_map/dynamic_update_slice | solution.py:25
  271.2 3.7 %dynamic_update_slice.124 = bf16[1152,768]{0,1:T(8,128)(2,1)} dynamic-update-slice(bf16[1152,768]{0,1:T(8,128)(2,1)} %dynamic_update_slice.123, bf16[72,768]{0,1:T(8,128)(2,1)S(1)} %copy.47, s32[]{:T(128)S(6)} %select_n.227, s32[]{:T(128)} %constant.159.clone.1) | dynamic-update-slice | bytes 221188 | tf_op jit(solution)/shard_map/dynamic_update_slice | solution.py:30
  275.1 3.7 %dynamic_update_slice.125 = bf16[1152,768]{0,1:T(8,128)(2,1)} dynamic-update-slice(bf16[1152,768]{0,1:T(8,128)(2,1)} %dynamic_update_slice.124, bf16[72,768]{0,1:T(8,128)(2,1)S(1)} %copy.48, s32[]{:T(128)S(6)} %select_n.229, s32[]{:T(128)} %constant.159.clone.1) | dynamic-update-slice | bytes 221188 | tf_op jit(solution)/shard_map/dynamic_update_slice | solution.py:25
  279.9 3.7 %dynamic_update_slice.126 = bf16[1152,768]{0,1:T(8,128)(2,1)} dynamic-update-slice(bf16[1152,768]{0,1:T(8,128)(2,1)} %dynamic_update_slice.125, bf16[72,768]{0,1:T(8,128)(2,1)S(1)} %copy.49, s32[]{:T(128)S(6)} %select_n.231, s32[]{:T(128)} %constant.159.clone.1) | dynamic-update-slice | bytes 221188 | tf_op jit(solution)/shard_map/dynamic_update_slice | solution.py:30
  284.7 3.7 %dynamic_update_slice.127 = bf16[1152,768]{0,1:T(8,128)(2,1)} dynamic-update-slice(bf16[1152,768]{0,1:T(8,128)(2,1)} %dynamic_update_slice.126, bf16[72,768]{0,1:T(8,128)(2,1)S(1)} %copy.50, s32[]{:T(128)S(6)} %select_n.233, s32[]{:T(128)} %constant.159.clone.1) | dynamic-update-slice | bytes 221188 | tf_op jit(solution)/shard_map/dynamic_update_slice | solution.py:25
  292.4 3.9 %copy.53 = bf16[1152,768]{0,1:T(8,128)(2,1)} copy(bf16[1152,768]{1,0:T(8,128)(2,1)} %all-gather.5.cloned.1.call-done) | data formatting | bytes 3538944 | tf_op jit(solution)/shard_map/all_gather | solution.py:76
  296.3 3.0 fusion.10
  (164 shorter events, 52.5 us)
Async XLA Ops:
  7.2 141.2 %copy-start = (bf16[768,1536]{1,0:T(8,128)(2,1)S(1)}, bf16[768,1536]{1,0:T(8,128)(2,1)}, u32[]{:S(2)}) copy-start(bf16[768,1536]{1,0:T(8,128)(2,1)} %param.15) | copy-start | bytes 7077892
  7.2 5.6 %copy-start.5 = (bf16[72,1536]{1,0:T(8,128)(2,1)S(1)}, bf16[72,1536]{1,0:T(8,128)(2,1)}, u32[]{:S(2)}) copy-start(bf16[72,1536]{1,0:T(8,128)(2,1)} %param.8) | copy-start | bytes 663556
  7.2 134.3 %all-gather.3.cloned.1.call-start = ((), (), s32[]{:S(2)}) async-start(), calls=%async_computation | async-start | bytes 1880064 | tf_op jit(solution)/shard_map/all_gather | solution.py:76
  15.7 276.7 %all-gather.5.cloned.1.call-start = ((), (), s32[]{:S(2)}) async-start(), calls=%async_computation.1 | async-start | bytes 1880064 | tf_op jit(solution)/shard_map/all_gather | solution.py:76
  15.7 46.9 %copy-start.1 = (bf16[1536,768]{1,0:T(8,128)(2,1)S(1)}, bf16[1536,768]{1,0:T(8,128)(2,1)}, u32[]{:S(2)}) copy-start(bf16[1536,768]{1,0:T(8,128)(2,1)} %param.12) | copy-start | bytes 7077892
  18.1 8.1 %collective-permute-start = (bf16[72,768]{1,0:T(8,128)(2,1)S(1)}, bf16[72,768]{1,0:T(8,128)(2,1)S(1)}, u32[]{:S(2)}, u32[]{:S(2)}) collective-permute-start(bf16[72,768]{1,0:T(8,128)(2,1)S(1)} %convolution_convert_fusion.4), channel_id=1, source_target_pairs={{0,1},{1,2},{2,3},{3,4},{4,5},{5,6},{6,7},{7,8},{8,9},{9,10},{10,1... | collective-permute-start | bytes 331784 | tf_op jit(solution)/shard_map/ppermute | solution.py:24
  18.7 7.5 %collective-permute-start.1 = (bf16[72,768]{1,0:T(8,128)(2,1)S(1)}, bf16[72,768]{1,0:T(8,128)(2,1)S(1)}, u32[]{:S(2)}, u32[]{:S(2)}) collective-permute-start(bf16[72,768]{1,0:T(8,128)(2,1)S(1)} %convolution_convert_fusion.4), channel_id=1, source_target_pairs={{0,15},{1,0},{2,1},{3,2},{4,3},{5,4},{6,5},{7,6},{8,7},{9,8},{10,9... | collective-permute-start | bytes 331784 | tf_op jit(solution)/shard_map/ppermute | solution.py:29
  26.2 8.3 %collective-permute-start.2 = (bf16[72,768]{1,0:T(8,128)(2,1)S(1)}, bf16[72,768]{1,0:T(8,128)(2,1)S(1)}, u32[]{:S(2)}, u32[]{:S(2)}) collective-permute-start(bf16[72,768]{1,0:T(8,128)(2,1)S(1)} %collective-permute-done), channel_id=1, source_target_pairs={{0,1},{1,2},{2,3},{3,4},{4,5},{5,6},{6,7},{7,8},{8,9},{9,10},{10,1... | collective-permute-start | bytes 331784 | tf_op jit(solution)/shard_map/ppermute | solution.py:24
  26.2 8.3 %collective-permute-start.3 = (bf16[72,768]{1,0:T(8,128)(2,1)S(1)}, bf16[72,768]{1,0:T(8,128)(2,1)S(1)}, u32[]{:S(2)}, u32[]{:S(2)}) collective-permute-start(bf16[72,768]{1,0:T(8,128)(2,1)S(1)} %collective-permute-done.1), channel_id=1, source_target_pairs={{0,15},{1,0},{2,1},{3,2},{4,3},{5,4},{6,5},{7,6},{8,7},{9,8},{10,9... | collective-permute-start | bytes 331784 | tf_op jit(solution)/shard_map/ppermute | solution.py:29
  34.5 7.0 %collective-permute-start.4 = (bf16[72,768]{1,0:T(8,128)(2,1)S(1)}, bf16[72,768]{1,0:T(8,128)(2,1)S(1)}, u32[]{:S(2)}, u32[]{:S(2)}) collective-permute-start(bf16[72,768]{1,0:T(8,128)(2,1)S(1)} %collective-permute-done.2), channel_id=1, source_target_pairs={{0,1},{1,2},{2,3},{3,4},{4,5},{5,6},{6,7},{7,8},{8,9},{9,10},{10,1... | collective-permute-start | bytes 331784 | tf_op jit(solution)/shard_map/ppermute | solution.py:24
  34.5 7.0 %collective-permute-start.5 = (bf16[72,768]{1,0:T(8,128)(2,1)S(1)}, bf16[72,768]{1,0:T(8,128)(2,1)S(1)}, u32[]{:S(2)}, u32[]{:S(2)}) collective-permute-start(bf16[72,768]{1,0:T(8,128)(2,1)S(1)} %collective-permute-done.3), channel_id=1, source_target_pairs={{0,15},{1,0},{2,1},{3,2},{4,3},{5,4},{6,5},{7,6},{8,7},{9,8},{10,9... | collective-permute-start | bytes 331784 | tf_op jit(solution)/shard_map/ppermute | solution.py:29
  41.5 21.2 %copy-start.7 = (bf16[72,768]{1,0:T(8,128)(2,1)}, bf16[72,768]{1,0:T(8,128)(2,1)S(1)}, u32[]{:S(2)}) copy-start(bf16[72,768]{1,0:T(8,128)(2,1)S(1)} %collective-permute-done.4) | copy-start | bytes 331780
  41.5 7.0 %collective-permute-start.6 = (bf16[72,768]{1,0:T(8,128)(2,1)S(1)}, bf16[72,768]{1,0:T(8,128)(2,1)S(1)}, u32[]{:S(2)}, u32[]{:S(2)}) collective-permute-start(bf16[72,768]{1,0:T(8,128)(2,1)S(1)} %collective-permute-done.4), channel_id=1, source_target_pairs={{0,1},{1,2},{2,3},{3,4},{4,5},{5,6},{6,7},{7,8},{8,9},{9,10},{10,1... | collective-permute-start | bytes 331784 | tf_op jit(solution)/shard_map/ppermute | solution.py:24
  41.5 21.1 %copy-start.9 = (bf16[72,768]{1,0:T(8,128)(2,1)}, bf16[72,768]{1,0:T(8,128)(2,1)S(1)}, u32[]{:S(2)}) copy-start(bf16[72,768]{1,0:T(8,128)(2,1)S(1)} %collective-permute-done.5) | copy-start | bytes 331780
  41.5 7.0 %collective-permute-start.7 = (bf16[72,768]{1,0:T(8,128)(2,1)S(1)}, bf16[72,768]{1,0:T(8,128)(2,1)S(1)}, u32[]{:S(2)}, u32[]{:S(2)}) collective-permute-start(bf16[72,768]{1,0:T(8,128)(2,1)S(1)} %collective-permute-done.5), channel_id=1, source_target_pairs={{0,15},{1,0},{2,1},{3,2},{4,3},{5,4},{6,5},{7,6},{8,7},{9,8},{10,9... | collective-permute-start | bytes 331784 | tf_op jit(solution)/shard_map/ppermute | solution.py:29
  48.4 14.1 %copy-start.11 = (bf16[72,768]{1,0:T(8,128)(2,1)}, bf16[72,768]{1,0:T(8,128)(2,1)S(1)}, u32[]{:S(2)}) copy-start(bf16[72,768]{1,0:T(8,128)(2,1)S(1)} %collective-permute-done.6) | copy-start | bytes 331780
  48.4 7.0 %collective-permute-start.8 = (bf16[72,768]{1,0:T(8,128)(2,1)S(1)}, bf16[72,768]{1,0:T(8,128)(2,1)S(1)}, u32[]{:S(2)}, u32[]{:S(2)}) collective-permute-start(bf16[72,768]{1,0:T(8,128)(2,1)S(1)} %collective-permute-done.6), channel_id=1, source_target_pairs={{0,1},{1,2},{2,3},{3,4},{4,5},{5,6},{6,7},{7,8},{8,9},{9,10},{10,1... | collective-permute-start | bytes 331784 | tf_op jit(solution)/shard_map/ppermute | solution.py:24
  48.4 14.1 %copy-start.13 = (bf16[72,768]{1,0:T(8,128)(2,1)}, bf16[72,768]{1,0:T(8,128)(2,1)S(1)}, u32[]{:S(2)}) copy-start(bf16[72,768]{1,0:T(8,128)(2,1)S(1)} %collective-permute-done.7) | copy-start | bytes 331780
  48.5 8.8 %collective-permute-start.9 = (bf16[72,768]{1,0:T(8,128)(2,1)S(1)}, bf16[72,768]{1,0:T(8,128)(2,1)}, u32[]{:S(2)}, u32[]{:S(2)}) collective-permute-start(bf16[72,768]{1,0:T(8,128)(2,1)S(1)} %collective-permute-done.7), channel_id=1, source_target_pairs={{0,15},{1,0},{2,1},{3,2},{4,3},{5,4},{6,5},{7,6},{8,7},{9,8},{10,9... | collective-permute-start | bytes 331784 | tf_op jit(solution)/shard_map/ppermute | solution.py:29
  55.4 7.1 %copy-start.15 = (bf16[72,768]{1,0:T(8,128)(2,1)}, bf16[72,768]{1,0:T(8,128)(2,1)S(1)}, u32[]{:S(2)}) copy-start(bf16[72,768]{1,0:T(8,128)(2,1)S(1)} %collective-permute-done.8) | copy-start | bytes 331780
  55.4 7.1 %collective-permute-start.10 = (bf16[72,768]{1,0:T(8,128)(2,1)S(1)}, bf16[72,768]{1,0:T(8,128)(2,1)}, u32[]{:S(2)}, u32[]{:S(2)}) collective-permute-start(bf16[72,768]{1,0:T(8,128)(2,1)S(1)} %collective-permute-done.8), channel_id=1, source_target_pairs={{0,1},{1,2},{2,3},{3,4},{4,5},{5,6},{6,7},{7,8},{8,9},{9,10},{10,1... | collective-permute-start | bytes 331784 | tf_op jit(solution)/shard_map/ppermute | solution.py:24
  57.3 12.5 %collective-permute-start.11 = (bf16[72,768]{1,0:T(8,128)(2,1)}, bf16[72,768]{1,0:T(8,128)(2,1)}, u32[]{:S(2)}, u32[]{:S(2)}) collective-permute-start(bf16[72,768]{1,0:T(8,128)(2,1)} %collective-permute-done.9), channel_id=1, source_target_pairs={{0,15},{1,0},{2,1},{3,2},{4,3},{5,4},{6,5},{7,6},{8,7},{9,8},{10,9... | collective-permute-start | bytes 331784 | tf_op jit(solution)/shard_map/ppermute | solution.py:29
  62.5 11.4 %collective-permute-start.12 = (bf16[72,768]{1,0:T(8,128)(2,1)}, bf16[72,768]{1,0:T(8,128)(2,1)}, u32[]{:S(2)}, u32[]{:S(2)}) collective-permute-start(bf16[72,768]{1,0:T(8,128)(2,1)} %collective-permute-done.10), channel_id=1, source_target_pairs={{0,1},{1,2},{2,3},{3,4},{4,5},{5,6},{6,7},{7,8},{8,9},{9,10},{10,1... | collective-permute-start | bytes 331784 | tf_op jit(solution)/shard_map/ppermute | solution.py:24
  66.4 22.9 %copy-start.8 = (bf16[72,768]{1,0:T(8,128)(2,1)S(1)}, bf16[72,768]{1,0:T(8,128)(2,1)}, u32[]{:S(2)}) copy-start(bf16[72,768]{1,0:T(8,128)(2,1)} %copy-done.7) | copy-start | bytes 331780
  69.7 58.3 %collective-permute-start.13 = (bf16[72,768]{1,0:T(8,128)(2,1)}, bf16[72,768]{1,0:T(8,128)(2,1)}, u32[]{:S(2)}, u32[]{:S(2)}) collective-permute-start(bf16[72,768]{1,0:T(8,128)(2,1)} %collective-permute-done.11), channel_id=1, source_target_pairs={{0,15},{1,0},{2,1},{3,2},{4,3},{5,4},{6,5},{7,6},{8,7},{9,8},{10,9... | collective-permute-start | bytes 331784 | tf_op jit(solution)/shard_map/ppermute | solution.py:29
  73.9 58.9 %collective-permute-start.14 = (bf16[72,768]{1,0:T(8,128)(2,1)}, bf16[72,768]{1,0:T(8,128)(2,1)}, u32[]{:S(2)}, u32[]{:S(2)}) collective-permute-start(bf16[72,768]{1,0:T(8,128)(2,1)} %collective-permute-done.12), channel_id=1, source_target_pairs={{0,1},{1,2},{2,3},{3,4},{4,5},{5,6},{6,7},{7,8},{8,9},{9,10},{10,1... | collective-permute-start | bytes 331784 | tf_op jit(solution)/shard_map/ppermute | solution.py:24
  74.1 19.0 %copy-start.10 = (bf16[72,768]{1,0:T(8,128)(2,1)S(1)}, bf16[72,768]{1,0:T(8,128)(2,1)}, u32[]{:S(2)}) copy-start(bf16[72,768]{1,0:T(8,128)(2,1)} %copy-done.9) | copy-start | bytes 331780
  77.5 19.6 %copy-start.12 = (bf16[72,768]{1,0:T(8,128)(2,1)S(1)}, bf16[72,768]{1,0:T(8,128)(2,1)}, u32[]{:S(2)}) copy-start(bf16[72,768]{1,0:T(8,128)(2,1)} %copy-done.11) | copy-start | bytes 331780
  81.5 19.5 %copy-start.14 = (bf16[72,768]{1,0:T(8,128)(2,1)S(1)}, bf16[72,768]{1,0:T(8,128)(2,1)}, u32[]{:S(2)}) copy-start(bf16[72,768]{1,0:T(8,128)(2,1)} %copy-done.13) | copy-start | bytes 331780
  85.4 19.4 %copy-start.16 = (bf16[72,768]{1,0:T(8,128)(2,1)S(1)}, bf16[72,768]{1,0:T(8,128)(2,1)}, u32[]{:S(2)}) copy-start(bf16[72,768]{1,0:T(8,128)(2,1)} %copy-done.15) | copy-start | bytes 331780
  139.7 1.3 copy-start.4
  148.4 8.4 %copy-start.6 = (bf16[72,1536]{1,0:T(8,128)(2,1)S(1)}, bf16[72,1536]{1,0:T(8,128)(2,1)}, u32[]{:S(2)}) copy-start(bf16[72,1536]{1,0:T(8,128)(2,1)} %param.9) | copy-start | bytes 663556
  149.0 7.8 %collective-permute-start.15 = (bf16[72,1536]{1,0:T(8,128)(2,1)S(1)}, bf16[72,1536]{1,0:T(8,128)(2,1)S(1)}, u32[]{:S(2)}, u32[]{:S(2)}) collective-permute-start(bf16[72,1536]{1,0:T(8,128)(2,1)S(1)} %get-tuple-element.7), channel_id=1, source_target_pairs={{4,0},{5,1},{6,2},{7,3},{8,4},{9,5},{10,6},{11,7},{12,8},{13,9},{1... | collective-permute-start | bytes 663560 | tf_op jit(solution)/shard_map/ppermute | solution.py:39
  157.0 5.3 %copy-start.31 = (f32[72]{0:T(128)}, f32[72]{0:T(128)S(1)}, u32[]{:S(2)}) copy-start(f32[72]{0:T(128)S(1)} %add_rsqrt_fusion) | copy-start | bytes 868
  159.9 54.4 %copy-start.2 = (bf16[1536,768]{1,0:T(8,128)(2,1)S(1)}, bf16[1536,768]{1,0:T(8,128)(2,1)}, u32[]{:S(2)}) copy-start(bf16[1536,768]{1,0:T(8,128)(2,1)} %param.12) | copy-start | bytes 7077892
  162.3 7.0 %collective-permute-start.16 = (bf16[72,768]{1,0:T(8,128)(2,1)S(1)}, bf16[72,768]{1,0:T(8,128)(2,1)S(1)}, u32[]{:S(2)}, u32[]{:S(2)}) collective-permute-start(bf16[72,768]{1,0:T(8,128)(2,1)S(1)} %convolution_convert_fusion.1), channel_id=1, source_target_pairs={{0,1},{1,2},{2,3},{3,4},{4,5},{5,6},{6,7},{7,8},{8,9},{9,10},{10,1... | collective-permute-start | bytes 331784 | tf_op jit(solution)/shard_map/ppermute | solution.py:24
  162.4 7.0 %collective-permute-start.17 = (bf16[72,768]{1,0:T(8,128)(2,1)S(1)}, bf16[72,768]{1,0:T(8,128)(2,1)S(1)}, u32[]{:S(2)}, u32[]{:S(2)}) collective-permute-start(bf16[72,768]{1,0:T(8,128)(2,1)S(1)} %convolution_convert_fusion.1), channel_id=1, source_target_pairs={{0,15},{1,0},{2,1},{3,2},{4,3},{5,4},{6,5},{7,6},{8,7},{9,8},{10,9... | collective-permute-start | bytes 331784 | tf_op jit(solution)/shard_map/ppermute | solution.py:29
  169.3 44.6 %copy-start.20 = (bf16[72,768]{1,0:T(8,128)(2,1)}, bf16[72,768]{1,0:T(8,128)(2,1)S(1)}, u32[]{:S(2)}) copy-start(bf16[72,768]{1,0:T(8,128)(2,1)S(1)} %collective-permute-done.16) | copy-start | bytes 331780
  169.3 7.3 %collective-permute-start.18 = (bf16[72,768]{1,0:T(8,128)(2,1)S(1)}, bf16[72,768]{1,0:T(8,128)(2,1)S(1)}, u32[]{:S(2)}, u32[]{:S(2)}) collective-permute-start(bf16[72,768]{1,0:T(8,128)(2,1)S(1)} %collective-permute-done.16), channel_id=1, source_target_pairs={{0,1},{1,2},{2,3},{3,4},{4,5},{5,6},{6,7},{7,8},{8,9},{9,10},{10,1... | collective-permute-start | bytes 331784 | tf_op jit(solution)/shard_map/ppermute | solution.py:24
  169.4 45.0 %copy-start.17 = (bf16[72,768]{1,0:T(8,128)(2,1)}, bf16[72,768]{1,0:T(8,128)(2,1)S(1)}, u32[]{:S(2)}) copy-start(bf16[72,768]{1,0:T(8,128)(2,1)S(1)} %collective-permute-done.17) | copy-start | bytes 331780
  169.4 7.3 %collective-permute-start.19 = (bf16[72,768]{1,0:T(8,128)(2,1)S(1)}, bf16[72,768]{1,0:T(8,128)(2,1)S(1)}, u32[]{:S(2)}, u32[]{:S(2)}) collective-permute-start(bf16[72,768]{1,0:T(8,128)(2,1)S(1)} %collective-permute-done.17), channel_id=1, source_target_pairs={{0,15},{1,0},{2,1},{3,2},{4,3},{5,4},{6,5},{7,6},{8,7},{9,8},{10,9... | collective-permute-start | bytes 331784 | tf_op jit(solution)/shard_map/ppermute | solution.py:29
  176.6 37.4 %copy-start.19 = (bf16[72,768]{1,0:T(8,128)(2,1)}, bf16[72,768]{1,0:T(8,128)(2,1)S(1)}, u32[]{:S(2)}) copy-start(bf16[72,768]{1,0:T(8,128)(2,1)S(1)} %collective-permute-done.18) | copy-start | bytes 331780
  176.6 7.0 %collective-permute-start.20 = (bf16[72,768]{1,0:T(8,128)(2,1)S(1)}, bf16[72,768]{1,0:T(8,128)(2,1)S(1)}, u32[]{:S(2)}, u32[]{:S(2)}) collective-permute-start(bf16[72,768]{1,0:T(8,128)(2,1)S(1)} %collective-permute-done.18), channel_id=1, source_target_pairs={{0,1},{1,2},{2,3},{3,4},{4,5},{5,6},{6,7},{7,8},{8,9},{9,10},{10,1... | collective-permute-start | bytes 331784 | tf_op jit(solution)/shard_map/ppermute | solution.py:24
  176.6 37.3 %copy-start.21 = (bf16[72,768]{1,0:T(8,128)(2,1)}, bf16[72,768]{1,0:T(8,128)(2,1)S(1)}, u32[]{:S(2)}) copy-start(bf16[72,768]{1,0:T(8,128)(2,1)S(1)} %collective-permute-done.19) | copy-start | bytes 331780
  176.6 7.0 %collective-permute-start.21 = (bf16[72,768]{1,0:T(8,128)(2,1)S(1)}, bf16[72,768]{1,0:T(8,128)(2,1)S(1)}, u32[]{:S(2)}, u32[]{:S(2)}) collective-permute-start(bf16[72,768]{1,0:T(8,128)(2,1)S(1)} %collective-permute-done.19), channel_id=1, source_target_pairs={{0,15},{1,0},{2,1},{3,2},{4,3},{5,4},{6,5},{7,6},{8,7},{9,8},{10,9... | collective-permute-start | bytes 331784 | tf_op jit(solution)/shard_map/ppermute | solution.py:29
  183.6 30.4 %copy-start.22 = (bf16[72,768]{1,0:T(8,128)(2,1)}, bf16[72,768]{1,0:T(8,128)(2,1)S(1)}, u32[]{:S(2)}) copy-start(bf16[72,768]{1,0:T(8,128)(2,1)S(1)} %collective-permute-done.20) | copy-start | bytes 331780
  183.6 9.1 %collective-permute-start.22 = (bf16[72,768]{1,0:T(8,128)(2,1)S(1)}, bf16[72,768]{1,0:T(8,128)(2,1)S(1)}, u32[]{:S(2)}, u32[]{:S(2)}) collective-permute-start(bf16[72,768]{1,0:T(8,128)(2,1)S(1)} %collective-permute-done.20), channel_id=1, source_target_pairs={{0,1},{1,2},{2,3},{3,4},{4,5},{5,6},{6,7},{7,8},{8,9},{9,10},{10,1... | collective-permute-start | bytes 331784 | tf_op jit(solution)/shard_map/ppermute | solution.py:24
  183.6 30.4 %copy-start.23 = (bf16[72,768]{1,0:T(8,128)(2,1)}, bf16[72,768]{1,0:T(8,128)(2,1)S(1)}, u32[]{:S(2)}) copy-start(bf16[72,768]{1,0:T(8,128)(2,1)S(1)} %collective-permute-done.21) | copy-start | bytes 331780
  183.6 9.1 %collective-permute-start.23 = (bf16[72,768]{1,0:T(8,128)(2,1)S(1)}, bf16[72,768]{1,0:T(8,128)(2,1)S(1)}, u32[]{:S(2)}, u32[]{:S(2)}) collective-permute-start(bf16[72,768]{1,0:T(8,128)(2,1)S(1)} %collective-permute-done.21), channel_id=1, source_target_pairs={{0,15},{1,0},{2,1},{3,2},{4,3},{5,4},{6,5},{7,6},{8,7},{9,8},{10,9... | collective-permute-start | bytes 331784 | tf_op jit(solution)/shard_map/ppermute | solution.py:29
  192.7 21.3 %copy-start.25 = (bf16[72,768]{1,0:T(8,128)(2,1)}, bf16[72,768]{1,0:T(8,128)(2,1)S(1)}, u32[]{:S(2)}) copy-start(bf16[72,768]{1,0:T(8,128)(2,1)S(1)} %collective-permute-done.22) | copy-start | bytes 331780
  192.7 7.4 %collective-permute-start.24 = (bf16[72,768]{1,0:T(8,128)(2,1)S(1)}, bf16[72,768]{1,0:T(8,128)(2,1)S(1)}, u32[]{:S(2)}, u32[]{:S(2)}) collective-permute-start(bf16[72,768]{1,0:T(8,128)(2,1)S(1)} %collective-permute-done.22), channel_id=1, source_target_pairs={{0,1},{1,2},{2,3},{3,4},{4,5},{5,6},{6,7},{7,8},{8,9},{9,10},{10,1... | collective-permute-start | bytes 331784 | tf_op jit(solution)/shard_map/ppermute | solution.py:24
  192.7 21.3 %copy-start.26 = (bf16[72,768]{1,0:T(8,128)(2,1)}, bf16[72,768]{1,0:T(8,128)(2,1)S(1)}, u32[]{:S(2)}) copy-start(bf16[72,768]{1,0:T(8,128)(2,1)S(1)} %collective-permute-done.23) | copy-start | bytes 331780
  192.7 7.4 %collective-permute-start.25 = (bf16[72,768]{1,0:T(8,128)(2,1)S(1)}, bf16[72,768]{1,0:T(8,128)(2,1)S(1)}, u32[]{:S(2)}, u32[]{:S(2)}) collective-permute-start(bf16[72,768]{1,0:T(8,128)(2,1)S(1)} %collective-permute-done.23), channel_id=1, source_target_pairs={{0,15},{1,0},{2,1},{3,2},{4,3},{5,4},{6,5},{7,6},{8,7},{9,8},{10,9... | collective-permute-start | bytes 331784 | tf_op jit(solution)/shard_map/ppermute | solution.py:29
  200.1 13.9 %copy-start.27 = (bf16[72,768]{1,0:T(8,128)(2,1)}, bf16[72,768]{1,0:T(8,128)(2,1)S(1)}, u32[]{:S(2)}) copy-start(bf16[72,768]{1,0:T(8,128)(2,1)S(1)} %collective-permute-done.24) | copy-start | bytes 331780
  200.1 7.0 %collective-permute-start.26 = (bf16[72,768]{1,0:T(8,128)(2,1)S(1)}, bf16[72,768]{1,0:T(8,128)(2,1)S(1)}, u32[]{:S(2)}, u32[]{:S(2)}) collective-permute-start(bf16[72,768]{1,0:T(8,128)(2,1)S(1)} %collective-permute-done.24), channel_id=1, source_target_pairs={{0,1},{1,2},{2,3},{3,4},{4,5},{5,6},{6,7},{7,8},{8,9},{9,10},{10,1... | collective-permute-start | bytes 331784 | tf_op jit(solution)/shard_map/ppermute | solution.py:24
  200.1 13.9 %copy-start.28 = (bf16[72,768]{1,0:T(8,128)(2,1)}, bf16[72,768]{1,0:T(8,128)(2,1)S(1)}, u32[]{:S(2)}) copy-start(bf16[72,768]{1,0:T(8,128)(2,1)S(1)} %collective-permute-done.25) | copy-start | bytes 331780
  200.1 7.0 %collective-permute-start.27 = (bf16[72,768]{1,0:T(8,128)(2,1)S(1)}, bf16[72,768]{1,0:T(8,128)(2,1)}, u32[]{:S(2)}, u32[]{:S(2)}) collective-permute-start(bf16[72,768]{1,0:T(8,128)(2,1)S(1)} %collective-permute-done.25), channel_id=1, source_target_pairs={{0,15},{1,0},{2,1},{3,2},{4,3},{5,4},{6,5},{7,6},{8,7},{9,8},{10,9... | collective-permute-start | bytes 331784 | tf_op jit(solution)/shard_map/ppermute | solution.py:29
  207.1 6.9 %copy-start.30 = (bf16[72,768]{1,0:T(8,128)(2,1)}, bf16[72,768]{1,0:T(8,128)(2,1)S(1)}, u32[]{:S(2)}) copy-start(bf16[72,768]{1,0:T(8,128)(2,1)S(1)} %collective-permute-done.26) | copy-start | bytes 331780
  207.1 6.9 %collective-permute-start.28 = (bf16[72,768]{1,0:T(8,128)(2,1)S(1)}, bf16[72,768]{1,0:T(8,128)(2,1)S(1)}, u32[]{:S(2)}, u32[]{:S(2)}) collective-permute-start(bf16[72,768]{1,0:T(8,128)(2,1)S(1)} %collective-permute-done.26), channel_id=1, source_target_pairs={{0,1},{1,2},{2,3},{3,4},{4,5},{5,6},{6,7},{7,8},{8,9},{9,10},{10,1... | collective-permute-start | bytes 331784 | tf_op jit(solution)/shard_map/ppermute | solution.py:24
  207.1 71.7 %collective-permute-start.29 = (bf16[72,768]{1,0:T(8,128)(2,1)}, bf16[72,768]{1,0:T(8,128)(2,1)}, u32[]{:S(2)}, u32[]{:S(2)}) collective-permute-start(bf16[72,768]{1,0:T(8,128)(2,1)} %collective-permute-done.27), channel_id=1, source_target_pairs={{0,15},{1,0},{2,1},{3,2},{4,3},{5,4},{6,5},{7,6},{8,7},{9,8},{10,9... | collective-permute-start | bytes 331784 | tf_op jit(solution)/shard_map/ppermute | solution.py:29
  214.0 69.6 %collective-permute-start.30 = (bf16[72,768]{1,0:T(8,128)(2,1)S(1)}, bf16[72,768]{1,0:T(8,128)(2,1)}, u32[]{:S(2)}, u32[]{:S(2)}) collective-permute-start(bf16[72,768]{1,0:T(8,128)(2,1)S(1)} %collective-permute-done.28), channel_id=1, source_target_pairs={{0,1},{1,2},{2,3},{3,4},{4,5},{5,6},{6,7},{7,8},{8,9},{9,10},{10,1... | collective-permute-start | bytes 331784 | tf_op jit(solution)/shard_map/ppermute | solution.py:24
  215.7 8.9 %copy-start.18 = (bf16[72,768]{1,0:T(8,128)(2,1)S(1)}, bf16[72,768]{1,0:T(8,128)(2,1)}, u32[]{:S(2)}) copy-start(bf16[72,768]{1,0:T(8,128)(2,1)} %copy-done.17) | copy-start | bytes 331780
  224.8 18.2 %copy-start.24 = (bf16[72,768]{1,0:T(8,128)(2,1)S(1)}, bf16[72,768]{1,0:T(8,128)(2,1)}, u32[]{:S(2)}) copy-start(bf16[72,768]{1,0:T(8,128)(2,1)} %copy-done.23) | copy-start | bytes 331780
  243.2 18.2 %copy-start.29 = (bf16[72,768]{1,0:T(8,128)(2,1)S(1)}, bf16[72,768]{1,0:T(8,128)(2,1)}, u32[]{:S(2)}) copy-start(bf16[72,768]{1,0:T(8,128)(2,1)} %copy-done.28) | copy-start | bytes 331780
  (1 other events, 1.3 us)
Sparse Core Ops, SparseCore 0:
  15.8 46.4 all-gather.2
  160.0 41.0 all-gather.4
